TPU v7x, 32 devices: a whole 2x2x4 slice. The times are simulated.
32 devices in a mesh: dp: 8 (over y, x, core), vocab: 4 (over z).
Axes of the slice: x: 2, y: 2, z: 4, core: 2. Of those that a mesh axis runs over, the one named last changes fastest.
Arguments:
- hidden_current: bfloat16 [256, 4096], P(('dp', 'vocab'))
- hidden_proximal: bfloat16 [256, 4096], P(('dp', 'vocab'))
- head_current: bfloat16 [4096, 128256], P(None, ('dp', 'vocab'))
- head_proximal: bfloat16 [4096, 128256], P(None, ('dp', 'vocab'))
- targets: int32 [256], P(('dp', 'vocab')), may hold values from 0 to 128255
- loss_mask: int32 [256], P(('dp', 'vocab')), may hold values from 0 to 1, as said below
- lengths: int32 [32], P(('dp', 'vocab')), may hold values from 1 to 8
- behavior_logprob: float32 [256], P(('dp', 'vocab')), may hold values from -14 to -10
- advantages: float32 [256], P(('dp', 'vocab')), may hold values from -6 to 6
Outputs:
- token_loss: float32 [256], P(('dp', 'vocab'))
- current_logprob: float32 [256], P(('dp', 'vocab'))
- stats: float32 [3], replicated
Inputs may be any that keep to these rules, and one draw needn't show every extreme that they name: `loss_mask`: 1 at the first position of every sequence's window.
All inputs are finite; a program needn't handle non-finite values.
Results may differ from a plain program's by a relative error of at most 0.0003.
Values may be sent and summed in bfloat16 or wider, within the bound.
A program may use at most 128 MiB of HBM per device.

v0:
```python
import jax
import jax.numpy as jnp
from jax import lax
from jax.sharding import PartitionSpec as P

POSITIONS = 8


CLIP_EPS = 0.2
WEIGHT_CAP = 5.0


def column_stats(logits, wanted, first_col, with_entropy):
    peak = jnp.max(logits, axis=1)
    weights = jnp.exp(logits - peak[:, None])
    total = jnp.sum(weights, axis=1)
    columns = first_col + lax.broadcasted_iota(jnp.int32, logits.shape, 1)
    picked = jnp.sum(jnp.where(columns == wanted[:, None], logits, jnp.float32(0.0)), axis=1)
    if with_entropy:
        moment = jnp.sum(weights * logits, axis=1)
        return [peak, total, moment, picked]
    return [peak, total, picked]


def token_terms(logp_current, logp_proximal, entropy, advantages, behavior, live):
    ratio = jnp.exp(logp_current - logp_proximal)
    clipped = jnp.clip(ratio, 1.0 - CLIP_EPS, 1.0 + CLIP_EPS)
    surrogate = jnp.maximum(-advantages * ratio, -advantages * clipped)
    weight = jnp.minimum(jnp.exp(logp_proximal - behavior), WEIGHT_CAP)
    return (surrogate * weight * live, weight * live, entropy * live)


def local(
    hidden_current,
    hidden_proximal,
    head_current,
    head_proximal,
    targets,
    loss_mask,
    lengths,
    behavior_logprob,
    advantages,
):
    tok_dev = targets.shape[0]
    first_col = lax.axis_index(("dp", "vocab")) * head_current.shape[1]
    row_start = lax.axis_index(("dp", "vocab")) * tok_dev
    all_targets = lax.all_gather(targets, ("dp", "vocab"), axis=0, tiled=True)
    place = lax.broadcasted_iota(jnp.int32, (lengths.shape[0], POSITIONS), 1)
    live = ((place < lengths[:, None]).reshape(-1) & (loss_mask == 1)).astype(jnp.float32)
    spread_adv, spread_behav, spread_live = (
        lax.all_gather(advantages, ("dp", "vocab"), axis=0, tiled=True),
        lax.all_gather(behavior_logprob, ("dp", "vocab"), axis=0, tiled=True),
        lax.all_gather(live, ("dp", "vocab"), axis=0, tiled=True),
    )
    stacked = jnp.stack([hidden_current, hidden_proximal])
    pieces = lax.all_gather(stacked, ("dp", "vocab"), axis=1, tiled=True)
    logits = jnp.dot(pieces[0], head_current, preferred_element_type=jnp.float32)
    proximal_logits = jnp.dot(pieces[1], head_proximal, preferred_element_type=jnp.float32)
    stats = jnp.concatenate(
        [
            jnp.stack(column_stats(logits, all_targets, first_col, True)),
            jnp.stack(column_stats(proximal_logits, all_targets, first_col, False)),
        ],
        axis=0,
    )
    peak_c, peak_p = lax.pmax((stats[0], stats[4]), ("dp", "vocab"))
    scale_c = jnp.exp(stats[0] - peak_c)
    scale_p = jnp.exp(stats[4] - peak_p)
    total_c, moment_c, picked_c, total_p, picked_p = lax.psum(
        (stats[1] * scale_c, stats[2] * scale_c, stats[3], stats[5] * scale_p, stats[6]),
        ("dp", "vocab"),
    )
    lse_c = peak_c + jnp.log(total_c)
    logp_c = picked_c - lse_c
    entropy = lse_c - moment_c / total_c
    logp_p = picked_p - (peak_p + jnp.log(total_p))

    def mine(values):
        return lax.dynamic_slice_in_dim(values, row_start, tok_dev)

    loss_all, weight_all, ent_all = token_terms(
        logp_c, logp_p, entropy, spread_adv, spread_behav, spread_live
    )
    loss_sum = jnp.sum(loss_all)
    weight_sum = jnp.sum(weight_all)
    ent_sum = jnp.sum(ent_all)
    count = jnp.sum(spread_live)
    token_loss = mine(loss_all)
    summary = jnp.stack([loss_sum / count, weight_sum / count, ent_sum / count])
    return (token_loss, mine(logp_c), summary)


def solution(mesh):
    placed = (
        P(("dp", "vocab"), None),
        P(("dp", "vocab"), None),
        P(None, ("dp", "vocab")),
        P(None, ("dp", "vocab")),
        P(("dp", "vocab")),
        P(("dp", "vocab")),
        P(("dp", "vocab")),
        P(("dp", "vocab")),
        P(("dp", "vocab")),
    )
    return jax.shard_map(
        local,
        mesh=mesh,
        in_specs=placed,
        out_specs=(P(("dp", "vocab")), P(("dp", "vocab")), P()),
        check_vma=False,
    )
```

profile of v0, /device:TPU:0, one launch (start us, length us, event | category | flops | bytes accessed | tf_op | source)
XLA Modules:
  0.0 205.9 jit_solution(5200341439054849451)
XLA Ops:
  7.2 0.0 all-gather.2.cloned.1.call-start
  7.2 1.5 pad_maximum_fusion
  8.7 0.0 all-gather.2.cloned.1.call-update
  9.4 0.9 dynamic-update-slice.1
  10.3 0.8 dynamic-update-slice
  11.1 0.8 dynamic-update-slice.2
  12.0 42.1 %all-reduce.1 = s32[256]{0:T(256)S(1)} all-reduce(s32[256]{0:T(256)S(1)} %dynamic-update-slice.1), channel_id=1, replica_groups=mesh['dp'=8,'vocab'=4] {'dp','vocab'}, use_global_device_ids=true, to_apply=%add.1 | all-reduce | flops 256 | bytes 2048
  54.1 0.7 fusion.6
  54.8 20.8 %all-gather.2.cloned.1.call-done = bf16[2,256,4096]{2,1,0:T(8,128)(2,1)} async-done(((bf16[2,8,4096]{2,1,0:T(8,128)(2,1)}), bf16[2,256,4096]{2,1,0:T(8,128)(2,1)}) %all-gather.2.cloned.1.call-update) | async-done | bytes 4194320 | tf_op jit(solution)/shard_map/all_gather | solution.py:56
  75.6 0.0 copy-start
  75.6 16.5 %fusion.11 = (f32[256]{0:T(256)S(1)}, f32[256,4008]{0,1:T(8,128)}) fusion(bf16[4096,4008]{0,1:T(8,128)(2,1)} %param.12, bf16[2,256,4096]{2,1,0:T(8,128)(2,1)} %all-gather.2.cloned.1.call-done), kind=kOutput, calls=%fused_computation.29 | convolution fusion | flops 8406411264 | bytes 39035904 | tf_op jit(solution)/shard_map/dot_general | solution.py:58
  92.1 0.0 copy-done
  92.1 16.4 %fusion.12 = (f32[256]{0:T(256)S(1)}, f32[256,4008]{0,1:T(8,128)}) fusion(bf16[4096,4008]{0,1:T(8,128)(2,1)} %param.11, bf16[2,256,4096]{2,1,0:T(8,128)(2,1)S(1)} %copy-done), kind=kOutput, calls=%fused_computation.30 | convolution fusion | flops 8406411264 | bytes 39035904 | tf_op jit(solution)/shard_map/dot_general | solution.py:57
  108.5 39.0 %all-reduce.5 = (f32[256]{0:T(256)S(1)}, f32[256]{0:T(256)S(1)}) all-reduce(f32[256]{0:T(256)S(1)} %get-tuple-element.34, f32[256]{0:T(256)S(1)} %get-tuple-element.32), channel_id=1, replica_groups=mesh['dp'=8,'vocab'=4] {'dp','vocab'}, use_global_device_ids=true, to_apply=%region_3.4 | all-reduce | flops 512 | bytes 4096 | tf_op jit(solution)/shard_map/pmax | solution.py:66
  147.6 5.1 %exponential_reduce_fusion = (f32[256]{0:T(256)S(1)}, f32[256]{0:T(256)S(1)}, f32[256]{0:T(256)S(1)}, f32[256]{0:T(256)S(1)}, f32[256]{0:T(256)S(1)}) fusion(f32[256,4008]{0,1:T(8,128)} %get-tuple-element.33, f32[256]{0:T(256)S(1)} %get-tuple-element.32, s32[256]{0:T(256)S(1)} %all-reduce.1, s32[4008]{0:T(1024)S(1)} %iota_add_fusion, ...), kind=kLoop, calls=%fused_computation.5 | loop fusion | flops 11285248 | bytes 8232608 | tf_op jit(solution)/shard_map/reduce_sum | solution.py:16
  152.7 40.1 %all-reduce.4 = (f32[256]{0:T(256)S(1)}, f32[256]{0:T(256)S(1)}, f32[256]{0:T(256)S(1)}, f32[256]{0:T(256)S(1)}, f32[256]{0:T(256)S(1)}, /*index=5*/f32[256]{0:T(256)S(1)}, f32[256]{0:T(256)S(1)}, f32[256]{0:T(256)S(1)}) all-reduce(f32[256]{0:T(256)S(1)} %fusion.6, ...), channel_id=1, replica_groups=mesh['dp'=8,'vocab'=4] {'dp','vocab'}, use_global_device_ids=true, to_apply=%add.3 | all-reduce | flops 2048 | bytes 16384
  192.8 0.6 multiply_reduce_fusion.2
  197.3 0.6 dynamic_slice.7
  197.9 0.6 dynamic_slice.6
  198.5 0.6 pad_maximum_fusion.1
  (6 shorter events, 0.0 us)
Async XLA Ops:
  7.2 68.4 %all-gather.2.cloned.1.call-start = ((), (), s32[]{:S(2)}) async-start(), calls=%async_computation | async-start | bytes 4325376 | tf_op jit(solution)/shard_map/all_gather | solution.py:56
  75.6 16.5 %copy-start = (bf16[2,256,4096]{2,1,0:T(8,128)(2,1)S(1)}, bf16[2,256,4096]{2,1,0:T(8,128)(2,1)}, u32[]{:S(2)}) copy-start(bf16[2,256,4096]{2,1,0:T(8,128)(2,1)} %all-gather.2.cloned.1.call-done) | copy-start | bytes 12582916
Sparse Core Ops, SparseCore 0:
  11.0 64.5 all-gather.1
where the time goes:
time: 207 us; the launch traced here: 206 us
  blocking collectives  121 us (58%)
  matrix products  32.9 us (16%)
  waiting for transfers between devices  20.8 us (10%)
  between operations  18.6 us (9%)
  other arithmetic  8.6 us (4%)
  local copies, waits for them, and re-layouts  3.72 us (2%)
    unnamed x2, blocking collectives  82.2 us
    pmax x1, blocking collectives, local(): peak_c, peak_p = lax.pmax((stats[0], stats[4]), ('dp', 'vocab'))  39 us
    all_gather x1, waiting for transfers between devices, local(): pieces = lax.all_gather(stacked, ('dp', 'vocab'), axis=1, tiled=True)  20.8 us
    dot_general x1, matrix products, local(): jnp.dot(pieces[1], head_proximal, preferred_element_type=jnp.float32)  16.5 us
    dot_general x1, matrix products, local(): jnp.dot(pieces[0], head_current, preferred_element_type=jnp.float32)  16.4 us
    reduce_sum x1, other arithmetic, column_stats(): total = jnp.sum(weights, axis=1)  5.1 us
  transfers between devices with their start and end apart: 1, of which 1 were waited for; matrix products, arithmetic and copies ran while one was open for 2% of the time, Pallas kernels for 0%

commit v1 on v0

v1 whole, which is shorter than its diff:
```python
import functools

import jax
import jax.numpy as jnp
from jax import lax
from jax.experimental import pallas as pl
from jax.experimental.pallas import tpu as pltpu
from jax.sharding import PartitionSpec as P

POSITIONS = 8

CLIP_EPS = 0.2
WEIGHT_CAP = 5.0
AXES = ("dp", "vocab")
MESH = pl.DeviceIdType.MESH
LANES = 128
TILE = 512
BLOCK = 64
PARTS = 4
SLOTS = 6


def flip(value, mask):
    bit = 1
    out = value
    while bit <= mask:
        if mask & bit:
            out = out + bit * (1 - 2 * ((value // bit) % 2))
        bit *= 2
    return out


def kernel(
    n_dp,
    n_v,
    target_ref,
    mask_ref,
    length_ref,
    behavior_ref,
    advantage_ref,
    hid_c_ref,
    hid_p_ref,
    head_c_ref,
    head_p_ref,
    out_ref,
    slabs,
    held,
    tags,
    aux_ref,
    hid_t,
    acc,
    stat_out,
    stat_in,
    sum_out,
    sum_in,
    slab_sem,
    own_sem,
    send_sem,
    recv_sem,
    tag_send,
    tag_recv,
    stat_send,
    stat_recv,
    sum_send,
    sum_recv,
):
    dp, v = lax.axis_index("dp"), lax.axis_index("vocab")
    me = dp * n_v + v
    n_dev = n_dp * n_v
    n_q = n_dp // 2
    half = n_q * n_v
    rows, depth = hid_c_ref.shape
    cols = head_c_ref.shape[0]
    part = depth // PARTS
    padded, tokens = acc.shape
    first_col = me * cols
    heads = (head_c_ref, head_p_ref)
    hids = (hid_c_ref, hid_p_ref)
    steps = 2 * PARTS

    def device_of(slot):
        core, rest = divmod(slot, half)
        q, z = divmod(rest, n_v)
        return (flip(dp, q * 2 + core), flip(v, z))

    def slab_copy(i):
        policy, k = divmod(i, PARTS)
        return pltpu.make_async_copy(
            heads[policy].at[:, pl.ds(k * part, part)], slabs.at[i % SLOTS], slab_sem.at[i % SLOTS]
        )

    own = [pltpu.make_async_copy(hids[p], held.at[p, 0], own_sem.at[p]) for p in range(2)]
    barrier = pltpu.get_barrier_semaphore()
    for slot in range(1, n_dev):
        pl.semaphore_signal(barrier, inc=1, device_id=device_of(slot), device_id_type=MESH)
    for copy in own:
        copy.start()
    for i in range(min(SLOTS, steps)):
        slab_copy(i).start()

    lane = lax.broadcasted_iota(jnp.int32, (rows, LANES), 1)
    row = lax.broadcasted_iota(jnp.int32, (rows, LANES), 0)
    aux = jnp.zeros((rows, LANES), jnp.float32)
    for r in range(rows):
        live = jnp.where(
            r % POSITIONS < length_ref[r // POSITIONS], jnp.where(mask_ref[r] == 1, 1.0, 0.0), 0.0
        )
        values = (target_ref[r].astype(jnp.float32), advantage_ref[r], behavior_ref[r], live)
        for n, one in enumerate(values):
            aux = jnp.where((row == r) & (lane == n), one, aux)
    aux_ref[...] = aux
    own_tag = pltpu.make_async_copy(aux_ref, tags.at[0], own_sem.at[2])
    own_tag.start()
    pl.semaphore_wait(barrier, n_dev - 1)

    sent = []

    def send(src, dst, s_sem, r_sem, slot):
        copy = pltpu.make_async_remote_copy(
            src_ref=src, dst_ref=dst, send_sem=s_sem, recv_sem=r_sem,
            device_id=device_of(slot), device_id_type=MESH,
        )
        copy.start()
        sent.append(copy)
        return copy

    bits = [1 << b for b in range(n_q.bit_length() - 1)]
    arrivals = {}

    def view(i, lo, count):
        if i is None:
            return tags.at[pl.ds(lo, count)]
        policy, k = divmod(i, PARTS)
        return held.at[policy, pl.ds(lo, count), :, pl.ds(k * part, part)]

    def message(i, lo_src, lo_dst, count, number, slot):
        s_sem = tag_send.at[number] if i is None else send_sem.at[i, number]
        r_sem = tag_recv.at[number] if i is None else recv_sem.at[i, number]
        copy = send(view(i, lo_src, count), view(i, lo_dst, count), s_sem, r_sem, slot)
        arrivals[(i, number)] = copy

    def landed(i, number):
        arrivals[(i, number)].wait_recv()

    def order_of(i):
        return bits if i is None or i % 2 == 0 else bits[::-1]

    def number_of(group):
        return n_v - 1 + group - 1

    def last_dim(order, group):
        return max(k for k, m in enumerate(order) if group & m)

    def groups_of_phase(order):
        groups = sorted(range(1, n_q), key=lambda g: (last_dim(order, g), bin(g).count("1"), g))
        return groups

    def forward(i, group):
        order = order_of(i)
        start = 0 if group == 0 else last_dim(order, group) + 1
        for k in range(start, len(order)):
            other = group ^ order[k]
            message(i, group * n_v, other * n_v, n_v, number_of(other), order[k] * n_v)

    def phase(i, j):
        order = order_of(i)
        groups = groups_of_phase(order)
        if j == 0:
            for z in range(1, n_v):
                message(i, 0, z, 1, z - 1, z)
        elif j == 1:
            for z in range(1, n_v):
                landed(i, z - 1)
            forward(i, 0)
        elif j <= len(bits):
            for g in groups:
                if last_dim(order, g) == j - 2:
                    landed(i, number_of(g))
                    forward(i, g)
        elif j == len(bits) + 1:
            for g in groups:
                if last_dim(order, g) == j - 2:
                    landed(i, number_of(g))
            message(i, 0, half, half, half - 1, half)
        else:
            landed(i, half - 1)

    last = len(bits) + 2
    for copy in own + [own_tag]:
        copy.wait()
    for i in range(steps):
        phase(i, 0)
        if i == 0:
            phase(None, 0)

    def step(t):
        for i in range(steps):
            j = t - i
            if 1 <= j <= last:
                phase(i, j)
                if i == 0:
                    phase(None, j)

    neg = float(jnp.finfo(jnp.float32).min)
    if padded > cols:
        edge = cols // 8 * 8
        acc[edge:, :] = jnp.full((padded - edge, tokens), neg, jnp.float32)

    full = cols // TILE

    def compute(i):
        policy, k = divmod(i, PARTS)
        slab_copy(i).wait()
        slab = slabs.at[i % SLOTS]
        piece = held[policy, :, :, k * part:(k + 1) * part]
        hid_t[...] = piece.astype(jnp.float32).reshape(tokens, part).T.astype(jnp.bfloat16)

        def tile(lo, width):
            at = pl.ds(lo, width)
            value = jnp.dot(slab[at, :], hid_t[...], preferred_element_type=jnp.float32)
            if k:
                value = value + acc[at, :]
            acc[at, :] = value

        @pl.loop(0, full)
        def _(n):
            tile(pl.multiple_of(n * TILE, TILE), TILE)

        if cols > full * TILE:
            tile(full * TILE, cols - full * TILE)
        if i + SLOTS < steps:
            slab_copy(i + SLOTS).start()

    def softmax(with_entropy):
        blocks = padded // BLOCK
        subs = BLOCK // 8
        width = min(tokens, 256)
        results = []
        for lo in range(0, tokens, width):
            here = slice(lo, lo + width)
            wanted = tags[pl.ds(lo // rows, width // rows)].reshape(width, LANES).T[0:1, :]
            wanted = wanted.astype(jnp.int32) - first_col
            wanted = jnp.where((wanted >= 0) & (wanted < cols), wanted, -1)
            wanted = wanted - lax.broadcasted_iota(jnp.int32, (8, width), 0)

            def largest(b, peak):
                base = pl.multiple_of(b * BLOCK, BLOCK)
                block = [acc[pl.ds(base + 8 * n, 8), here] for n in range(subs)]
                while len(block) > 1:
                    block = [jnp.maximum(x, y) for x, y in zip(block[::2], block[1::2])]
                return jnp.maximum(peak, block[0])

            peak = lax.fori_loop(0, blocks, largest, jnp.full((8, width), neg, jnp.float32))
            peak = jnp.max(peak, axis=0, keepdims=True)

            def summed(b, carry):
                total, moment, picked = carry
                base = pl.multiple_of(b * BLOCK, BLOCK)
                for n in range(subs):
                    value = acc[pl.ds(base + 8 * n, 8), here]
                    weight = jnp.exp(value - peak)
                    total = total + weight
                    if with_entropy:
                        moment = moment + weight * value
                    picked = picked + jnp.where(wanted == base + 8 * n, value, 0.0)
                return total, moment, picked

            zero = jnp.zeros((8, width), jnp.float32)
            sums = lax.fori_loop(0, blocks, summed, (zero, zero, zero))
            total, moment, picked = [jnp.sum(x, axis=0, keepdims=True) for x in sums]
            results.append((peak, total, picked, moment))
        return [jnp.concatenate([r[n] for r in results], axis=1) for n in range(4)]

    for t in range(1, last):
        step(t)
    for i in range(steps):
        step(last + i)
        compute(i)
        if i == PARTS - 1:
            found = softmax(True)
        elif i == steps - 1:
            found = found + softmax(False)
    table = jnp.concatenate(found + [jnp.zeros((LANES - 8, tokens), jnp.float32)], axis=0)
    stat_out[...] = table.T

    back = []
    for slot in range(1, n_dev):
        back.append(send(
            stat_out.at[pl.ds(slot * rows, rows)], stat_in.at[slot],
            stat_send.at[slot], stat_recv.at[slot], slot,
        ))
    stat_in[0] = stat_out[0:rows, :]
    for copy in back:
        copy.wait_recv()
    stats = stat_in[...]

    def column(n):
        return stats[:, :, n:n + 1]

    peak_c = jnp.max(column(0), axis=0, keepdims=True)
    peak_p = jnp.max(column(4), axis=0, keepdims=True)
    scale_c = jnp.exp(column(0) - peak_c)
    scale_p = jnp.exp(column(4) - peak_p)
    total_c = jnp.sum(column(1) * scale_c, axis=0)
    moment_c = jnp.sum(column(3) * scale_c, axis=0)
    picked_c = jnp.sum(column(2), axis=0)
    total_p = jnp.sum(column(5) * scale_p, axis=0)
    picked_p = jnp.sum(column(6), axis=0)
    lse_c = peak_c[0] + jnp.log(total_c)
    logp_c = picked_c - lse_c
    entropy = lse_c - moment_c / total_c
    logp_p = picked_p - (peak_p[0] + jnp.log(total_p))
    aux = aux_ref[...]
    advantages, behavior, live = aux[:, 1:2], aux[:, 2:3], aux[:, 3:4]
    ratio = jnp.exp(logp_c - logp_p)
    clipped = jnp.clip(ratio, 1.0 - CLIP_EPS, 1.0 + CLIP_EPS)
    surrogate = jnp.maximum(-advantages * ratio, -advantages * clipped)
    weight = jnp.minimum(jnp.exp(logp_p - behavior), WEIGHT_CAP)
    loss = surrogate * weight * live

    terms = jnp.where(lane == 2, loss, 0.0)
    terms = jnp.where(lane == 3, weight * live, terms)
    terms = jnp.where(lane == 4, entropy * live, terms)
    terms = jnp.where(lane == 5, live, terms)
    mine = jnp.sum(terms, axis=0, keepdims=True)
    sum_out[...] = mine
    sums = []
    for slot in range(1, n_dev):
        sums.append(send(sum_out, sum_in.at[me], sum_send.at[slot], sum_recv.at[slot], slot))
    sum_in[me] = mine
    for copy in sums:
        copy.wait_recv()
    whole = jnp.sum(sum_in[...], axis=0)
    count = whole[:, 5:6]
    result = whole / count
    result = jnp.where(lane == 0, loss, jnp.broadcast_to(result, (rows, LANES)))
    out_ref[...] = jnp.where(lane == 1, logp_c, result)
    for copy in sent:
        copy.wait_send()


def local(
    n_dp,
    n_v,
    hidden_current,
    hidden_proximal,
    head_current,
    head_proximal,
    targets,
    loss_mask,
    lengths,
    behavior_logprob,
    advantages,
):
    rows, depth = hidden_current.shape
    cols = head_current.shape[1]
    n_dev = n_dp * n_v
    tokens = n_dev * rows
    padded = -(-cols // BLOCK) * BLOCK
    messages = n_dev // 2
    vmem = pl.BlockSpec(memory_space=pltpu.VMEM)
    smem = pl.BlockSpec(memory_space=pltpu.SMEM)
    anywhere = pl.BlockSpec(memory_space=pl.ANY)
    dma = pltpu.SemaphoreType.DMA
    out = pl.pallas_call(
        functools.partial(kernel, n_dp, n_v),
        out_shape=jax.ShapeDtypeStruct((rows, LANES), jnp.float32),
        in_specs=[smem] * 5 + [anywhere, anywhere, anywhere, anywhere],
        out_specs=vmem,
        scratch_shapes=[
            pltpu.VMEM((SLOTS, cols, depth // PARTS), jnp.bfloat16),
            pltpu.VMEM((2, n_dev, rows, depth), jnp.bfloat16),
            pltpu.VMEM((n_dev, rows, LANES), jnp.float32),
            pltpu.VMEM((rows, LANES), jnp.float32),
            pltpu.VMEM((depth // PARTS, tokens), jnp.bfloat16),
            pltpu.VMEM((padded, tokens), jnp.float32),
            pltpu.VMEM((tokens, LANES), jnp.float32),
            pltpu.VMEM((n_dev, rows, LANES), jnp.float32),
            pltpu.VMEM((1, LANES), jnp.float32),
            pltpu.VMEM((n_dev, 1, LANES), jnp.float32),
            dma((SLOTS,)),
            dma((3,)),
            dma((2 * PARTS, messages)),
            dma((2 * PARTS, messages)),
            dma((messages,)),
            dma((messages,)),
            dma((n_dev,)),
            dma((n_dev,)),
            dma((n_dev,)),
            dma((n_dev,)),
        ],
        compiler_params=pltpu.CompilerParams(
            collective_id=0, has_side_effects=True, vmem_limit_bytes=67043328
        ),
    )(
        targets, loss_mask, lengths, behavior_logprob, advantages,
        hidden_current, hidden_proximal, head_current.T, head_proximal.T,
    )
    return (out[:, 0], out[:, 1], out[0, 2:5])


def solution(mesh):
    placed = (
        P(AXES, None),
        P(AXES, None),
        P(None, AXES),
        P(None, AXES),
        P(AXES),
        P(AXES),
        P(AXES),
        P(AXES),
        P(AXES),
    )
    return jax.shard_map(
        functools.partial(local, mesh.shape["dp"], mesh.shape["vocab"]),
        mesh=mesh,
        in_specs=placed,
        out_specs=(P(AXES), P(AXES), P()),
        check_vma=False,
    )
```

time: 207 us -> 94.1 us (0.45)
  blocking collectives: 121 us -> 0 us
  Pallas kernels: 0 us -> 89.8 us
  matrix products: 32.9 us -> 0 us
  waiting for transfers between devices: 20.8 us -> 0 us
  between operations: 18.6 us -> 1.29 us
  other arithmetic: 8.6 us -> 0 us
    pallas_call x0 -> x1, Pallas kernels: none -> 89.8 us  [local(): pl.pallas_call(functools.partial(kernel, n_dp, n_v), out_shape=jax.ShapeD...]
    unnamed x2 -> x0, blocking collectives: 82.2 us -> none
    pmax x1 -> x0, blocking collectives: 39 us -> none  [local(): peak_c, peak_p = lax.pmax((stats[0], stats[4]), ('dp', 'vocab'))]
    dot_general x2 -> x0, matrix products: 32.9 us -> none  [the longest x1 16.5 us: local(): jnp.dot(pieces[1], head_proximal, preferred_element_type=jnp.float32)]
    all_gather x1 -> x0, waiting for transfers between devices: 20.8 us -> none  [local(): pieces = lax.all_gather(stacked, ('dp', 'vocab'), axis=1, tiled=True)]
    reduce_sum x2 -> x0, other arithmetic: 5.72 us -> none  [the longest x1 5.1 us: column_stats(): total = jnp.sum(weights, axis=1)]
    unnamed x9 -> x0, local copies, waits for them, and re-layouts: 2.54 us -> none
    another operation x2 -> x0, other arithmetic: 2.11 us -> none  [the longest x1 1.53 us: local(): stacked = jnp.stack([hidden_current, hidden_proximal])]
  transfers between devices with their start and end apart: 1 -> 0, of which waited for: 1 -> 0; matrix products, arithmetic and copies ran while one was open for 2% -> 0% of each run, Pallas kernels for 0% -> 0%
where the time goes in v1:
time: 94.1 us; the launch traced here: 93.9 us
  Pallas kernels  89.8 us (95%)
  local copies, waits for them, and re-layouts  2.75 us (3%)
  between operations  1.29 us (1%)
    pallas_call x1, Pallas kernels, local(): pl.pallas_call(functools.partial(kernel, n_dp, n_v), out_shape=jax.ShapeD...  89.8 us

profile of v1, /device:TPU:0, one launch (start us, length us, event | category | flops | bytes accessed | tf_op | source)
XLA Modules:
  0.0 93.9 jit_solution(9595419012809259613)
XLA Ops:
  1.3 89.8 %shard_map.112 = f32[8,128]{1,0:T(8,128)} custom-call(s32[8]{0:T(128)} %target_ref.1, s32[8]{0:T(128)} %mask_ref.1, s32[1]{0:T(128)S(6)} %copy.12.length_ref, f32[8]{0:T(128)} %behavior_ref.1, f32[8]{0:T(128)} %advantage_ref.1, bf16[8,4096]{1,0:T(8,128)(2,1)} %hid_c_ref.1, bf16[8,4096]{1,0:T(8,128)(2,1)} %hid_p_ref.1, bf16[4008,4096]{1,0:T(8,128)(2,1)} %bitcast.4, ...), custom_call_target="tpu_custom_call" | custom-call | tf_op jit(solution)/shard_map/pallas_call | solution.py:365
  91.1 1.5 %slice_reduce_fusion = (f32[8]{0:T(128)}, f32[8]{0:T(128)}) fusion(f32[8,128]{1,0:T(8,128)} %shard_map.112), kind=kLoop, calls=%fused_computation | loop fusion | bytes 128 | tf_op jit(solution)/shard_map/slice | solution.py:399
  92.6 1.3 %slice_bitcast_fusion = f32[3]{0:T(128)} fusion(f32[8,128]{1,0:T(8,128)} %shard_map.112), kind=kLoop, calls=%fused_computation.2 | loop fusion | bytes 24 | tf_op jit(solution)/shard_map/squeeze | solution.py:399

commit v2 on v1

--- a/solution.py
+++ b/solution.py
@@ -14,10 +14,11 @@
 AXES = ("dp", "vocab")
 MESH = pl.DeviceIdType.MESH
 LANES = 128
-TILE = 512
+TILE = 1024
 BLOCK = 64
 PARTS = 4
 SLOTS = 6
+STRIDE = 2
 
 
 def flip(value, mask):
@@ -89,7 +90,13 @@
             heads[policy].at[:, pl.ds(k * part, part)], slabs.at[i % SLOTS], slab_sem.at[i % SLOTS]
         )
 
-    own = [pltpu.make_async_copy(hids[p], held.at[p, 0], own_sem.at[p]) for p in range(2)]
+    own = [
+        pltpu.make_async_copy(
+            hids[p].at[:, pl.ds(k * part, part)], held.at[p, k, 0], own_sem.at[p * PARTS + k]
+        )
+        for p in range(2)
+        for k in range(PARTS)
+    ]
     barrier = pltpu.get_barrier_semaphore()
     for slot in range(1, n_dev):
         pl.semaphore_signal(barrier, inc=1, device_id=device_of(slot), device_id_type=MESH)
@@ -109,7 +116,7 @@
         for n, one in enumerate(values):
             aux = jnp.where((row == r) & (lane == n), one, aux)
     aux_ref[...] = aux
-    own_tag = pltpu.make_async_copy(aux_ref, tags.at[0], own_sem.at[2])
+    own_tag = pltpu.make_async_copy(aux_ref, tags.at[0], own_sem.at[steps])
     own_tag.start()
     pl.semaphore_wait(barrier, n_dev - 1)
 
@@ -131,7 +138,7 @@
         if i is None:
             return tags.at[pl.ds(lo, count)]
         policy, k = divmod(i, PARTS)
-        return held.at[policy, pl.ds(lo, count), :, pl.ds(k * part, part)]
+        return held.at[policy, k, pl.ds(lo, count)]
 
     def message(i, lo_src, lo_dst, count, number, slot):
         s_sem = tag_send.at[number] if i is None else send_sem.at[i, number]
@@ -195,8 +202,8 @@
 
     def step(t):
         for i in range(steps):
-            j = t - i
-            if 1 <= j <= last:
+            j, rest = divmod(t - i, STRIDE)
+            if rest == 0 and 1 <= j <= last:
                 phase(i, j)
                 if i == 0:
                     phase(None, j)
@@ -212,7 +219,7 @@
         policy, k = divmod(i, PARTS)
         slab_copy(i).wait()
         slab = slabs.at[i % SLOTS]
-        piece = held[policy, :, :, k * part:(k + 1) * part]
+        piece = held[policy, k]
         hid_t[...] = piece.astype(jnp.float32).reshape(tokens, part).T.astype(jnp.bfloat16)
 
         def tile(lo, width):
@@ -271,10 +278,10 @@
             results.append((peak, total, picked, moment))
         return [jnp.concatenate([r[n] for r in results], axis=1) for n in range(4)]
 
-    for t in range(1, last):
+    for t in range(1, STRIDE * last):
         step(t)
     for i in range(steps):
-        step(last + i)
+        step(STRIDE * last + i)
         compute(i)
         if i == PARTS - 1:
             found = softmax(True)
@@ -369,7 +376,7 @@
         out_specs=vmem,
         scratch_shapes=[
             pltpu.VMEM((SLOTS, cols, depth // PARTS), jnp.bfloat16),
-            pltpu.VMEM((2, n_dev, rows, depth), jnp.bfloat16),
+            pltpu.VMEM((2, PARTS, n_dev, rows, depth // PARTS), jnp.bfloat16),
             pltpu.VMEM((n_dev, rows, LANES), jnp.float32),
             pltpu.VMEM((rows, LANES), jnp.float32),
             pltpu.VMEM((depth // PARTS, tokens), jnp.bfloat16),
@@ -379,7 +386,7 @@
             pltpu.VMEM((1, LANES), jnp.float32),
             pltpu.VMEM((n_dev, 1, LANES), jnp.float32),
             dma((SLOTS,)),
-            dma((3,)),
+            dma((2 * PARTS + 1,)),
             dma((2 * PARTS, messages)),
             dma((2 * PARTS, messages)),
             dma((messages,)),

time: 94.1 us -> 80.2 us (0.85)
  Pallas kernels: 89.8 us -> 75.8 us
    pallas_call x1, Pallas kernels: 89.8 us -> 75.8 us  [local(): pl.pallas_call(functools.partial(kernel, n_dp, n_v), out_shape=jax.ShapeD...]
where the time goes in v2:
time: 80.2 us; the launch traced here: 79.9 us
  Pallas kernels  75.8 us (95%)
  local copies, waits for them, and re-layouts  2.75 us (3%)
  between operations  1.29 us (2%)
    pallas_call x1, Pallas kernels, local(): pl.pallas_call(functools.partial(kernel, n_dp, n_v), out_shape=jax.ShapeD...  75.8 us

profile of v2, /device:TPU:0, one launch (start us, length us, event | category | flops | bytes accessed | tf_op | source)
XLA Modules:
  0.0 79.9 jit_solution(713240778191507268)
XLA Ops:
  1.3 75.8 %shard_map.112 = f32[8,128]{1,0:T(8,128)} custom-call(s32[8]{0:T(128)} %target_ref.1, s32[8]{0:T(128)} %mask_ref.1, s32[1]{0:T(128)S(6)} %copy.12.length_ref, f32[8]{0:T(128)} %behavior_ref.1, f32[8]{0:T(128)} %advantage_ref.1, bf16[8,4096]{1,0:T(8,128)(2,1)} %hid_c_ref.1, bf16[8,4096]{1,0:T(8,128)(2,1)} %hid_p_ref.1, bf16[4008,4096]{1,0:T(8,128)(2,1)} %bitcast.4, ...), custom_call_target="tpu_custom_call" | custom-call | tf_op jit(solution)/shard_map/pallas_call | solution.py:372
  77.1 1.5 %slice_reduce_fusion = (f32[8]{0:T(128)}, f32[8]{0:T(128)}) fusion(f32[8,128]{1,0:T(8,128)} %shard_map.112), kind=kLoop, calls=%fused_computation | loop fusion | bytes 128 | tf_op jit(solution)/shard_map/slice | solution.py:406
  78.6 1.3 %slice_bitcast_fusion = f32[3]{0:T(128)} fusion(f32[8,128]{1,0:T(8,128)} %shard_map.112), kind=kLoop, calls=%fused_computation.2 | loop fusion | bytes 24 | tf_op jit(solution)/shard_map/squeeze | solution.py:406
